TPU v7x, 256 devices: a whole 4x4x8 slice. The times are simulated.
256 devices in a mesh: dp: 16 (over y_lo, x, core), chan: 16 (over y_hi, z).
Axes of the slice: x: 4, y: 4 (y_hi: 2, y_lo: 2; y = y_hi * 2 + y_lo), z: 8, core: 2. Of those that a mesh axis runs over, the one named last changes fastest.
Arguments:
- anchors: bfloat16 [256, 128, 4096], P('dp', 'chan'), may hold values from -15 to 15
- views: bfloat16 [256, 128, 4096], P('dp', 'chan'), may hold values from -15 to 15
- dw_weight: float32 [128, 4], replicated, may hold values from -3 to 3
- pw_weight: bfloat16 [256, 128], replicated, may hold values from -0.5 to 0.5
- proj_weight: bfloat16 [256, 1024], replicated, may hold values from -0.375 to 0.375
- partner: int32 [256], P('dp'), may hold values from 0 to 255, each once
Outputs:
- loss: float32 [256], P('dp')
- grad_dw: float32 [128, 4], P('chan')
- grad_pw: float32 [256, 128], replicated
- grad_proj: float32 [256, 1024], P('chan', 'dp')
Inputs may be any that keep to these rules, and one draw needn't show every extreme that they name: `partner`: each view index appears exactly once.
All inputs are finite; a program needn't handle non-finite values.
Results may differ from a plain program's by a relative error of at most 0.0044.
Values may be sent and summed in bfloat16 or wider, within the bound.
No kernel may reach another device: no remote copies, remote signals or barrier semaphores. Data moves between devices by JAX's collectives and lax.ppermute only.
A program may use at most 192 MiB of HBM per device.

v0:
```python
import jax
import jax.numpy as jnp
from jax import lax
from jax.sharding import PartitionSpec as P

TAPS = 4
TAP_SPACING = 16
logit_scale = 16.0


def passed_along(value, axis, steps):
    count = lax.axis_size(axis)
    pairs = [(source, (source + steps) % count) for source in range(count)]
    return lax.ppermute(value, axis, pairs)


def depthwise(trace_block, dw_weight):
    widened = trace_block.astype(jnp.float32)
    length = trace_block.shape[2]
    running = jnp.zeros(widened.shape, jnp.float32)
    for tap_index in range(TAPS):
        offset_steps = tap_index * TAP_SPACING
        shifted = jnp.pad(
            widened[:, :, : length - offset_steps], ((0, 0), (0, 0), (offset_steps, 0))
        )
        running = running + dw_weight[None, :, tap_index, None] * shifted
    return running.astype(jnp.bfloat16)


def silu_slope(mixed):
    sigma = jax.nn.sigmoid(mixed)
    return sigma * (1.0 + mixed * (1.0 - sigma))


def kernel_terms(grad_conv, extended):
    rim_width = (TAPS - 1) * TAP_SPACING
    span_width = grad_conv.shape[2]
    columns = []
    for tap_index in range(TAPS):
        begin = rim_width - tap_index * TAP_SPACING
        window = extended[:, :, begin : begin + span_width]
        columns.append(
            jnp.einsum("nct,nct->c", grad_conv, window, preferred_element_type=jnp.float32)
        )
    return jnp.stack(columns, 1)


def block_scores(queries, key_rows, owner_index, partner, factor):
    logits = factor * lax.dot_general(
        queries, key_rows, (((1,), (1,)), ((), ())), preferred_element_type=jnp.float32
    )
    columns = owner_index * key_rows.shape[0] + jnp.arange(key_rows.shape[0], dtype=jnp.int32)
    matches = columns[None, :] == partner[:, None]
    return (logits, matches)


def body(anchors, views, dw_weight, pw_weight, proj_weight, partner):
    stacked = jnp.concatenate([anchors, views], 0)
    pair_count = anchors.shape[0]
    length = anchors.shape[2]
    chan_index = lax.axis_index("chan")
    chan_count = lax.axis_size("chan")
    cycle_index = lax.axis_index("dp")
    cycle_size = lax.axis_size("dp")
    rim_width = (TAPS - 1) * TAP_SPACING
    local_metrics = anchors.shape[1]
    local_kernel = lax.dynamic_slice_in_dim(dw_weight, chan_index * local_metrics, local_metrics, 0)
    conv_local = depthwise(stacked, local_kernel)
    conv_rows = lax.all_to_all(conv_local, "chan", split_axis=2, concat_axis=1, tiled=True)
    mixed = jnp.einsum("fc,nct->nft", pw_weight, conv_rows, preferred_element_type=jnp.float32)
    partial_pool = jnp.sum(jax.nn.silu(mixed), 2) / length
    conv_time, mixed, partial_pool = (conv_rows, mixed, partial_pool)
    pooled = lax.psum(partial_pool, "chan")
    pooled_bf = pooled.astype(jnp.bfloat16)
    embedding = jnp.dot(pooled_bf, proj_weight, preferred_element_type=jnp.float32)
    inverse = lax.rsqrt(jnp.mean(embedding * embedding, 1, keepdims=True) + 1e-06)
    unit_rows = embedding * inverse
    unit_bf = unit_rows.astype(jnp.bfloat16)
    queries = unit_bf[:pair_count]
    own_keys = unit_bf[pair_count:]
    factor = logit_scale / proj_weight.shape[1]

    def total_terms(key_rows, owner_index, totals, positive):
        logits, matches = block_scores(queries, key_rows, owner_index, partner, factor)
        totals = totals + jnp.sum(jnp.exp(logits - logit_scale), 1)
        positive = positive + jnp.sum(jnp.where(matches, logits, 0.0), 1)
        return (totals, positive)

    def first_turn(turn_index, loop_state):
        key_rows, totals, positive = loop_state
        owner_index = (cycle_index - turn_index) % cycle_size
        totals, positive = total_terms(key_rows, owner_index, totals, positive)
        key_rows = passed_along(key_rows, "dp", 1)
        return (key_rows, totals, positive)

    start_zero = jnp.zeros((pair_count,), jnp.float32)
    key_rows, totals, positive = lax.fori_loop(
        0, cycle_size - 1, first_turn, (own_keys, start_zero, start_zero)
    )
    totals, positive = total_terms(
        key_rows, (cycle_index - (cycle_size - 1)) % cycle_size, totals, positive
    )

    def grad_terms(key_rows, owner_index, carried, grad_query):
        logits, matches = block_scores(queries, key_rows, owner_index, partner, factor)
        coeffs = (
            jnp.exp(logits - logit_scale) / totals[:, None] - matches.astype(jnp.float32)
        ).astype(jnp.bfloat16)
        grad_query = grad_query + factor * jnp.dot(
            coeffs, key_rows, preferred_element_type=jnp.float32
        )
        carried = carried + factor * lax.dot_general(
            coeffs, queries, (((0,), (0,)), ((), ())), preferred_element_type=jnp.float32
        )
        return (carried, grad_query)

    def second_turn(turn_index, loop_state):
        key_rows, carried, grad_query = loop_state
        owner_index = (cycle_index - turn_index) % cycle_size
        carried, grad_query = grad_terms(key_rows, owner_index, carried, grad_query)
        key_rows = passed_along(key_rows, "dp", 1)
        carried = passed_along(carried, "dp", 1)
        return (key_rows, carried, grad_query)

    start_grads = jnp.zeros(own_keys.shape, jnp.float32)
    key_rows, carried, grad_query = lax.fori_loop(
        0, cycle_size - 1, second_turn, (own_keys, start_grads, start_grads)
    )
    carried, grad_query = grad_terms(
        key_rows, (cycle_index - (cycle_size - 1)) % cycle_size, carried, grad_query
    )
    grad_key = passed_along(carried, "dp", 1)
    losses = logit_scale + jnp.log(totals) - positive
    grad_unit = jnp.concatenate([grad_query, grad_key], 0)
    grad_embed = inverse * (
        grad_unit - unit_rows * jnp.mean(unit_rows * grad_unit, 1, keepdims=True)
    )
    grad_embed_bf = grad_embed.astype(jnp.bfloat16)
    filter_rows = proj_weight.shape[0] // chan_count
    pooled_rows = lax.dynamic_slice_in_dim(pooled_bf, chan_index * filter_rows, filter_rows, 1)
    proj_terms = lax.dot_general(
        pooled_rows, grad_embed_bf, (((0,), (0,)), ((), ())), preferred_element_type=jnp.float32
    )
    grad_proj = lax.psum_scatter(proj_terms, "dp", scatter_dimension=1, tiled=True)
    grad_pool = lax.dot_general(
        grad_embed_bf, proj_weight, (((1,), (1,)), ((), ())), preferred_element_type=jnp.float32
    )
    grad_mixed = (grad_pool[:, :, None] / length * silu_slope(mixed)).astype(jnp.bfloat16)
    mix_terms = jnp.einsum("nft,nct->fc", grad_mixed, conv_time, preferred_element_type=jnp.float32)
    grad_conv = jnp.einsum(
        "fc,nft->nct", pw_weight, grad_mixed, preferred_element_type=jnp.float32
    ).astype(jnp.bfloat16)
    grad_pw = lax.psum(mix_terms, ("dp", "chan"))
    grad_local = lax.all_to_all(grad_conv, "chan", split_axis=1, concat_axis=2, tiled=True)
    extended = jnp.pad(stacked, ((0, 0), (0, 0), (rim_width, 0)))
    kernel_part = kernel_terms(grad_local, extended)
    grad_dw = lax.psum(kernel_part, "dp")
    return (losses, grad_dw, grad_pw, grad_proj)


def solution(mesh):
    placed = (P("dp", "chan", None), P("dp", "chan", None), P(), P(), P(), P("dp"))
    return jax.shard_map(
        body,
        mesh=mesh,
        in_specs=placed,
        out_specs=(P("dp"), P("chan", None), P(), P("chan", "dp")),
        check_vma=False,
    )
```

profile of v0, /device:TPU:2, one launch (start us, length us, event | category | flops | bytes accessed | tf_op | source)
XLA Modules:
  0.0 708.4 jit_solution(9025586352325555345)
XLA Ops:
  10.7 7.9 %copy.34 = bf16[32,8,4096]{0,1,2:T(8,128)(2,1)} copy(bf16[32,8,4096]{2,1,0:T(8,128)(2,1)S(1)} %constant_dynamic-update-slice_fusion) | data formatting | bytes 4194304 | tf_op jit(solution)/shard_map/concatenate | solution.py:58
  18.6 10.5 %slice.49 = f32[32,8,4080]{0,1,2:T(8,128)} slice(bf16[32,8,4096]{0,1,2:T(8,128)(2,1)} %copy.34), slice={[0:32], [0:8], [0:4080]} | slice | bytes 8355840 | tf_op jit(solution)/shard_map/slice | solution.py:24
  30.5 6.0 slice.50
  36.5 6.0 slice.51
  42.5 23.1 %fusion.44 = bf16[4096,8,32]{2,1,0:T(8,128)(2,1)} fusion(f32[32,8,4048]{0,1,2:T(8,128)} %slice.51, f32[8]{0:T(128)S(1)} %get-tuple-element.488, f32[32,8,4064]{0,1,2:T(8,128)} %slice.50, f32[8]{0:T(128)S(1)} %get-tuple-element.489, f32[32,8,4080]{0,1,2:T(8,128)} %slice.49, f32[8]{0:T(128)S(1)} %get-tuple-element.490, bf16[32,8,4096]{0,1,2:T(8,128)(2,1)} %copy.34, ...), kind=kLoop, calls=%fused_computation.88 | loop fusion | flops 9437184 | bytes 16679040
  65.6 14.5 %reshape.59 = bf16[16,2,32768]{2,1,0:T(2,128)(2,1)} reshape(bf16[4096,8,32]{2,1,0:T(8,128)(2,1)} %fusion.44) | data formatting | bytes 4194304
  80.1 11.3 %all-to-all-start = ((bf16[16,2,32768]{2,1,0:T(2,128)(2,1)}), bf16[16,2,32768]{2,1,0:T(2,128)(2,1)}, u32[]{:S(2)}, u32[]{:S(2)}) async-start(bf16[16,2,32768]{2,1,0:T(2,128)(2,1)} %reshape.59), calls=%async_computation | async-start | bytes 4194304 | tf_op jit(solution)/shard_map/all_to_all | solution.py:69
  91.4 50.5 %all-to-all-done = bf16[16,2,32768]{2,1,0:T(2,128)(2,1)} async-done(((bf16[16,2,32768]{2,1,0:T(2,128)(2,1)}), bf16[16,2,32768]{2,1,0:T(2,128)(2,1)}, u32[]{:S(2)}, u32[]{:S(2)}) %all-to-all-start) | async-done | bytes 2097184 | tf_op jit(solution)/shard_map/all_to_all | solution.py:69
  141.9 12.9 %reshape.60 = bf16[4096,8,32]{2,1,0:T(8,128)(2,1)} reshape(bf16[16,2,32768]{2,1,0:T(2,128)(2,1)} %all-to-all-done) | data formatting | bytes 4194304
  154.8 10.5 %copy.36 = bf16[32,16,8,256]{3,2,1,0:T(8,128)(2,1)} copy(bf16[32,16,8,256]{0,2,3,1:T(8,128)(2,1)} %bitcast.123) | data formatting | bytes 4194304 | tf_op jit(solution)/shard_map/all_to_all | solution.py:69
  165.3 6.2 fusion.12
  171.5 74.3 %psum.21 = bf16[32,256]{1,0:T(8,128)(2,1)S(1)} all-reduce(f32[32,256]{1,0:T(8,128)S(1)} %broadcast_multiply_fusion), channel_id=1, replica_groups=mesh['dp'=16,'chan'=16] {'chan'}, use_global_device_ids=true, to_apply=%region_1.2 | all-reduce | flops 8192 | bytes 49152 | tf_op jit(solution)/shard_map/psum | solution.py:73
  246.3 74.0 %while.40 = (s32[]{:T(128)}, bf16[16,1024]{1,0:T(8,128)(2,1)S(1)}, f32[16]{0:T(128)S(1)}, f32[16]{0:T(128)S(1)}, bf16[16,1024]{1,0:T(8,128)(2,1)S(1)}, /*index=5...) while((s32[]{:T(128)}, bf16[16,1024]{1,0:T(8,128)(2,1)S(1)}, ...), condition=%wide.region_6.7_spmd.clone, body=%wide.region_3.6_spmd.clone.sunk | while | flops 525888 | bytes 263144 | solution.py:97
  260.4 5.3 collective-permute-done
  265.9 5.3 collective-permute-done
  271.3 5.3 collective-permute-done
  276.8 5.3 collective-permute-done
  282.2 5.3 collective-permute-done
  287.7 5.3 collective-permute-done
  293.2 5.3 collective-permute-done
  298.6 5.3 collective-permute-done
  304.1 5.3 collective-permute-done
  309.5 5.3 collective-permute-done
  315.0 5.3 collective-permute-done
  320.9 92.6 %while.41 = (s32[]{:T(128)}, bf16[16,1024]{1,0:T(8,128)(2,1)S(1)}, f32[16,1024]{1,0:T(8,128)S(1)}, f32[16,1024]{1,0:T(8,128)S(1)}, bf16[16,1024]{1,0:T(8,128)(2,...) while((s32[]{:T(128)}, bf16[16,1024]{1,0:T(8,128)(2,1)S(1)}, ...), condition=%wide.region_10.11_spmd.clone, body=%wide.region_9.10_spmd.clone.sunk | while | flops 1656608 | bytes 854104 | solution.py:126
  321.6 4.9 collective-permute-done.1
  414.2 5.6 collective-permute-done.3
  420.4 5.0 fusion.16
  440.3 4.8 fusion.25
  445.1 64.7 %reduce-scatter.4.cloned.1.call-done = f32[64,16]{1,0:T(8,128)} async-done(((f32[1024,16]{1,0:T(8,128)}), f32[64,16]{1,0:T(8,128)}) %reduce-scatter.4.cloned.1.call-update) | async-done | bytes 4112
  516.8 28.9 %psum.22 = f32[8,4]{0,1:T(4,128)} all-reduce(f32[8,4]{0,1:T(4,128)S(1)} %pad_maximum_fusion.1), channel_id=1, replica_groups=mesh['dp'=16,'chan'=16] {'dp'}, use_global_device_ids=true, to_apply=%region_12.13 | all-reduce | flops 32 | bytes 256 | tf_op jit(solution)/shard_map/psum | solution.py:157
  545.7 153.7 %all-reduce.6.cloned.1.call-done = f32[256,128]{1,0:T(8,128)} async-done(((f32[256,128]{1,0:T(8,128)}), f32[256,128]{1,0:T(8,128)}) %all-reduce.6.cloned.1.call-update) | async-done | bytes 131088 | tf_op jit(solution)/shard_map/psum | solution.py:153
  (264 shorter events, 133.1 us)
Async XLA Ops:
  80.1 61.8 %all-to-all-start = ((bf16[16,2,32768]{2,1,0:T(2,128)(2,1)}), bf16[16,2,32768]{2,1,0:T(2,128)(2,1)}, u32[]{:S(2)}, u32[]{:S(2)}) async-start(bf16[16,2,32768]{2,1,0:T(2,128)(2,1)} %reshape.59), calls=%async_computation | async-start | bytes 4194304 | tf_op jit(solution)/shard_map/all_to_all | solution.py:69
  260.2 5.4 collective-permute-start
  265.7 5.4 collective-permute-start
  271.2 5.4 collective-permute-start
  276.6 5.4 collective-permute-start
  282.1 5.4 collective-permute-start
  287.5 5.4 collective-permute-start
  293.0 5.4 collective-permute-start
  298.4 5.4 collective-permute-start
  303.9 5.4 collective-permute-start
  309.3 5.4 collective-permute-start
  314.8 5.4 collective-permute-start
  320.9 5.5 collective-permute-start.1
  321.4 5.9 collective-permute-start.2
  327.6 5.6 collective-permute-start.2
  333.4 5.9 collective-permute-start.2
  339.6 5.9 collective-permute-start.2
  345.8 5.9 collective-permute-start.2
  352.0 5.9 collective-permute-start.2
  358.2 5.9 collective-permute-start.2
  364.4 5.9 collective-permute-start.2
  370.5 5.9 collective-permute-start.2
  376.7 5.9 collective-permute-start.2
  382.9 5.9 collective-permute-start.2
  389.1 5.9 collective-permute-start.2
  395.3 5.9 collective-permute-start.2
  401.5 5.9 collective-permute-start.2
  407.7 5.9 collective-permute-start.2
  413.8 6.1 collective-permute-start.3
  434.6 76.7 %all-to-all-start.1 = ((bf16[32,128,256]{2,0,1:T(8,128)(2,1)}), bf16[32,128,256]{2,0,1:T(8,128)(2,1)}, u32[]{:S(2)}, u32[]{:S(2)}) async-start(bf16[32,128,256]{2,0,1:T(8,128)(2,1)} %copy.39), calls=%async_computation.1 | async-start | bytes 4194304 | tf_op jit(solution)/shard_map/all_to_all | solution.py:154
  439.0 70.8 %reduce-scatter.4.cloned.1.call-start = ((), (), s32[]{:S(2)}) async-start(), calls=%async_computation.4 | async-start | bytes 557056
  440.2 259.2 %all-reduce.6.cloned.1.call-start = ((), (), s32[]{:S(2)}) async-start(), calls=%async_computation.3 | async-start | bytes 262144 | tf_op jit(solution)/shard_map/psum | solution.py:153
  (24 other events, 502.4 us)
Sparse Core Ops, SparseCore 0:
  442.3 67.4 reduce-scatter.3
Sparse Core Ops, SparseCore 1:
  446.8 252.6 all-reduce.5
where the time goes:
time: 710 us; the launch traced here: 708 us
  waiting for transfers between devices  403 us (57%)
  blocking collectives  103 us (15%)
  local copies, waits for them, and re-layouts  84.8 us (12%)
  starting transfers between devices  43.8 us (6%)
  other arithmetic  32.1 us (5%)
  matrix products  24.8 us (3%)
  between operations  15.7 us (2%)
    psum x1, waiting for transfers between devices, body(): grad_pw = lax.psum(mix_terms, ('dp', 'chan'))  154 us
    ppermute x46, waiting for transfers between devices, passed_along(): return lax.ppermute(value, axis, pairs)  135 us
    psum x1, blocking collectives, body(): pooled = lax.psum(partial_pool, 'chan')  74.3 us
    unnamed x3, waiting for transfers between devices  64.7 us
    all_to_all x1, waiting for transfers between devices, body(): lax.all_to_all(conv_local, 'chan', split_axis=2, concat_axis=1, tiled=True)  50.5 us
    unnamed x18, local copies, waits for them, and re-layouts  35.1 us
    psum x1, blocking collectives, body(): grad_dw = lax.psum(kernel_part, 'dp')  28.9 us
    ppermute x46, starting transfers between devices, passed_along(): return lax.ppermute(value, axis, pairs)  28.1 us
  transfers between devices with their start and end apart: 50, of which 49 were waited for; matrix products, arithmetic and copies ran while one was open for 3% of the time, Pallas kernels for 0%

commit v1 on v0

--- a/solution.py
+++ b/solution.py
@@ -150,7 +150,7 @@
     grad_conv = jnp.einsum(
         "fc,nft->nct", pw_weight, grad_mixed, preferred_element_type=jnp.float32
     ).astype(jnp.bfloat16)
-    grad_pw = lax.psum(mix_terms, ("dp", "chan"))
+    grad_pw = lax.psum(lax.psum(mix_terms, "chan"), "dp")
     grad_local = lax.all_to_all(grad_conv, "chan", split_axis=1, concat_axis=2, tiled=True)
     extended = jnp.pad(stacked, ((0, 0), (0, 0), (rim_width, 0)))
     kernel_part = kernel_terms(grad_local, extended)

time: 710 us -> 739 us (1.041)
  waiting for transfers between devices: 403 us -> 433 us
    psum x1 -> x2, waiting for transfers between devices: 154 us -> 183 us  [body(): grad_pw = lax.psum(lax.psum(mix_terms, 'chan'), 'dp')]
    unnamed x3 -> x4, waiting for transfers between devices: 64.7 us -> 65 us
  transfers between devices with their start and end apart: 50 -> 51, of which waited for: 49 -> 50; matrix products, arithmetic and copies ran while one was open for 3% -> 3% of each run, Pallas kernels for 0% -> 0%
where the time goes in v1:
time: 739 us; the launch traced here: 734 us
  waiting for transfers between devices  433 us (59%)
  blocking collectives  98.2 us (13%)
  local copies, waits for them, and re-layouts  84.8 us (11%)
  starting transfers between devices  43.9 us (6%)
  other arithmetic  32.1 us (4%)
  matrix products  24.8 us (3%)
  between operations  15.7 us (2%)
    psum x2, waiting for transfers between devices, body(): grad_pw = lax.psum(lax.psum(mix_terms, 'chan'), 'dp')  183 us
    ppermute x46, waiting for transfers between devices, passed_along(): return lax.ppermute(value, axis, pairs)  135 us
    psum x1, blocking collectives, body(): pooled = lax.psum(partial_pool, 'chan')  74.3 us
    unnamed x4, waiting for transfers between devices  65 us
    all_to_all x1, waiting for transfers between devices, body(): lax.all_to_all(conv_local, 'chan', split_axis=2, concat_axis=1, tiled=True)  50.5 us
    unnamed x18, local copies, waits for them, and re-layouts  35.1 us
    ppermute x46, starting transfers between devices, passed_along(): return lax.ppermute(value, axis, pairs)  28.1 us
    psum x1, blocking collectives, body(): grad_dw = lax.psum(kernel_part, 'dp')  23.9 us
  transfers between devices with their start and end apart: 51, of which 50 were waited for; matrix products, arithmetic and copies ran while one was open for 3% of the time, Pallas kernels for 0%

profile of v1, /device:TPU:2, one launch (start us, length us, event | category | flops | bytes accessed | tf_op | source)
XLA Modules:
  0.0 733.5 jit_solution(12984944249497556484)
XLA Ops:
  10.7 7.9 %copy.34 = bf16[32,8,4096]{0,1,2:T(8,128)(2,1)} copy(bf16[32,8,4096]{2,1,0:T(8,128)(2,1)S(1)} %constant_dynamic-update-slice_fusion) | data formatting | bytes 4194304 | tf_op jit(solution)/shard_map/concatenate | solution.py:58
  18.6 10.5 %slice.49 = f32[32,8,4080]{0,1,2:T(8,128)} slice(bf16[32,8,4096]{0,1,2:T(8,128)(2,1)} %copy.34), slice={[0:32], [0:8], [0:4080]} | slice | bytes 8355840 | tf_op jit(solution)/shard_map/slice | solution.py:24
  30.5 6.0 slice.50
  36.5 6.0 slice.51
  42.5 23.1 %fusion.44 = bf16[4096,8,32]{2,1,0:T(8,128)(2,1)} fusion(f32[32,8,4048]{0,1,2:T(8,128)} %slice.51, f32[8]{0:T(128)S(1)} %get-tuple-element.488, f32[32,8,4064]{0,1,2:T(8,128)} %slice.50, f32[8]{0:T(128)S(1)} %get-tuple-element.489, f32[32,8,4080]{0,1,2:T(8,128)} %slice.49, f32[8]{0:T(128)S(1)} %get-tuple-element.490, bf16[32,8,4096]{0,1,2:T(8,128)(2,1)} %copy.34, ...), kind=kLoop, calls=%fused_computation.88 | loop fusion | flops 9437184 | bytes 16679040
  65.6 14.5 %reshape.59 = bf16[16,2,32768]{2,1,0:T(2,128)(2,1)} reshape(bf16[4096,8,32]{2,1,0:T(8,128)(2,1)} %fusion.44) | data formatting | bytes 4194304
  80.1 11.3 %all-to-all-start = ((bf16[16,2,32768]{2,1,0:T(2,128)(2,1)}), bf16[16,2,32768]{2,1,0:T(2,128)(2,1)}, u32[]{:S(2)}, u32[]{:S(2)}) async-start(bf16[16,2,32768]{2,1,0:T(2,128)(2,1)} %reshape.59), calls=%async_computation | async-start | bytes 4194304 | tf_op jit(solution)/shard_map/all_to_all | solution.py:69
  91.4 50.5 %all-to-all-done = bf16[16,2,32768]{2,1,0:T(2,128)(2,1)} async-done(((bf16[16,2,32768]{2,1,0:T(2,128)(2,1)}), bf16[16,2,32768]{2,1,0:T(2,128)(2,1)}, u32[]{:S(2)}, u32[]{:S(2)}) %all-to-all-start) | async-done | bytes 2097184 | tf_op jit(solution)/shard_map/all_to_all | solution.py:69
  141.9 12.9 %reshape.60 = bf16[4096,8,32]{2,1,0:T(8,128)(2,1)} reshape(bf16[16,2,32768]{2,1,0:T(2,128)(2,1)} %all-to-all-done) | data formatting | bytes 4194304
  154.8 10.5 %copy.36 = bf16[32,16,8,256]{3,2,1,0:T(8,128)(2,1)} copy(bf16[32,16,8,256]{0,2,3,1:T(8,128)(2,1)} %bitcast.123) | data formatting | bytes 4194304 | tf_op jit(solution)/shard_map/all_to_all | solution.py:69
  165.3 6.2 fusion.12
  171.5 74.3 %psum.28 = bf16[32,256]{1,0:T(8,128)(2,1)S(1)} all-reduce(f32[32,256]{1,0:T(8,128)S(1)} %broadcast_multiply_fusion), channel_id=1, replica_groups=mesh['dp'=16,'chan'=16] {'chan'}, use_global_device_ids=true, to_apply=%region_1.2 | all-reduce | flops 8192 | bytes 49152 | tf_op jit(solution)/shard_map/psum | solution.py:73
  246.3 74.0 %while.40 = (s32[]{:T(128)}, bf16[16,1024]{1,0:T(8,128)(2,1)S(1)}, f32[16]{0:T(128)S(1)}, f32[16]{0:T(128)S(1)}, bf16[16,1024]{1,0:T(8,128)(2,1)S(1)}, /*index=5...) while((s32[]{:T(128)}, bf16[16,1024]{1,0:T(8,128)(2,1)S(1)}, ...), condition=%wide.region_6.7_spmd.clone, body=%wide.region_3.6_spmd.clone.sunk | while | flops 525888 | bytes 263144 | solution.py:97
  260.4 5.3 collective-permute-done
  265.9 5.3 collective-permute-done
  271.3 5.3 collective-permute-done
  276.8 5.3 collective-permute-done
  282.2 5.3 collective-permute-done
  287.7 5.3 collective-permute-done
  293.2 5.3 collective-permute-done
  298.6 5.3 collective-permute-done
  304.1 5.3 collective-permute-done
  309.5 5.3 collective-permute-done
  315.0 5.3 collective-permute-done
  320.9 92.6 %while.41 = (s32[]{:T(128)}, bf16[16,1024]{1,0:T(8,128)(2,1)S(1)}, f32[16,1024]{1,0:T(8,128)S(1)}, f32[16,1024]{1,0:T(8,128)S(1)}, bf16[16,1024]{1,0:T(8,128)(2,...) while((s32[]{:T(128)}, bf16[16,1024]{1,0:T(8,128)(2,1)S(1)}, ...), condition=%wide.region_10.11_spmd.clone, body=%wide.region_9.10_spmd.clone.sunk | while | flops 1656608 | bytes 854104 | solution.py:126
  321.6 4.9 collective-permute-done.1
  414.2 5.6 collective-permute-done.3
  420.4 5.0 fusion.16
  445.1 64.9 %reduce-scatter.4.cloned.1.call-done = f32[64,16]{1,0:T(8,128)} async-done(((f32[1024,16]{1,0:T(8,128)}), f32[64,16]{1,0:T(8,128)}) %reduce-scatter.4.cloned.1.call-update) | async-done | bytes 4112
  511.5 98.1 %all-reduce.7.cloned.1.call-done = f32[256,128]{1,0:T(8,128)} async-done(((f32[256,128]{1,0:T(8,128)}), f32[256,128]{1,0:T(8,128)}) %all-reduce.7.cloned.1.call-update) | async-done | bytes 131088 | tf_op jit(solution)/shard_map/psum | solution.py:153
  615.2 23.9 %psum.29 = f32[8,4]{0,1:T(4,128)} all-reduce(f32[8,4]{0,1:T(4,128)S(1)} %pad_maximum_fusion.1), channel_id=1, replica_groups=mesh['dp'=16,'chan'=16] {'dp'}, use_global_device_ids=true, to_apply=%region_12.13 | all-reduce | flops 32 | bytes 256 | tf_op jit(solution)/shard_map/psum | solution.py:157
  639.1 85.4 %all-reduce.9.cloned.1.call-done = f32[256,128]{1,0:T(8,128)} async-done(((f32[256,128]{1,0:T(8,128)}), f32[256,128]{1,0:T(8,128)}) %all-reduce.9.cloned.1.call-update) | async-done | bytes 131088 | tf_op jit(solution)/shard_map/psum | solution.py:153
  (267 shorter events, 138.0 us)
Async XLA Ops:
  80.1 61.8 %all-to-all-start = ((bf16[16,2,32768]{2,1,0:T(2,128)(2,1)}), bf16[16,2,32768]{2,1,0:T(2,128)(2,1)}, u32[]{:S(2)}, u32[]{:S(2)}) async-start(bf16[16,2,32768]{2,1,0:T(2,128)(2,1)} %reshape.59), calls=%async_computation | async-start | bytes 4194304 | tf_op jit(solution)/shard_map/all_to_all | solution.py:69
  260.2 5.4 collective-permute-start
  265.7 5.4 collective-permute-start
  271.2 5.4 collective-permute-start
  276.6 5.4 collective-permute-start
  282.1 5.4 collective-permute-start
  287.5 5.4 collective-permute-start
  293.0 5.4 collective-permute-start
  298.4 5.4 collective-permute-start
  309.3 5.4 collective-permute-start
  314.8 5.4 collective-permute-start
  320.9 5.5 collective-permute-start.1
  321.4 5.9 collective-permute-start.2
  327.6 5.6 collective-permute-start.2
  333.4 5.9 collective-permute-start.2
  339.6 5.9 collective-permute-start.2
  345.8 5.9 collective-permute-start.2
  352.0 5.9 collective-permute-start.2
  358.2 5.9 collective-permute-start.2
  364.4 5.9 collective-permute-start.2
  370.5 5.9 collective-permute-start.2
  376.7 5.9 collective-permute-start.2
  382.9 5.9 collective-permute-start.2
  389.1 5.9 collective-permute-start.2
  395.3 5.9 collective-permute-start.2
  401.5 5.9 collective-permute-start.2
  407.7 5.9 collective-permute-start.2
  413.8 6.1 collective-permute-start.3
  434.6 175.1 %all-to-all-start.1 = ((bf16[32,128,256]{2,0,1:T(8,128)(2,1)}), bf16[32,128,256]{2,0,1:T(8,128)(2,1)}, u32[]{:S(2)}, u32[]{:S(2)}) async-start(bf16[32,128,256]{2,0,1:T(8,128)(2,1)} %copy.39), calls=%async_computation.1 | async-start | bytes 4194304 | tf_op jit(solution)/shard_map/all_to_all | solution.py:154
  439.0 71.1 %reduce-scatter.4.cloned.1.call-start = ((), (), s32[]{:S(2)}) async-start(), calls=%async_computation.5 | async-start | bytes 557056
  440.2 169.4 %all-reduce.7.cloned.1.call-start = ((), (), s32[]{:S(2)}) async-start(), calls=%async_computation.3 | async-start | bytes 262144 | tf_op jit(solution)/shard_map/psum | solution.py:153
  445.1 279.4 %all-reduce.9.cloned.1.call-start = ((), (), s32[]{:S(2)}) async-start(), calls=%async_computation.4 | async-start | bytes 262144 | tf_op jit(solution)/shard_map/psum | solution.py:153
  (25 other events, 507.8 us)
Sparse Core Ops, SparseCore 0:
  442.3 67.6 reduce-scatter.3
  609.7 114.7 all-reduce.8
Sparse Core Ops, SparseCore 1:
  445.2 164.4 all-reduce.6
